TPU v7x, 512 devices: a whole 4x8x8 slice. The times are simulated.
512 devices in a mesh: dp: 2 (over core), tensor: 4 (over x), expert: 64 (over y, z).
Axes of the slice: x: 4, y: 8, z: 8, core: 2. Of those that a mesh axis runs over, the one named last changes fastest.
Arguments:
- checkpoint: bfloat16 [16384, 2048], P(('dp', 'expert'), 'tensor'), may hold values from -6 to 6
- scales: float32 [16384], P(('dp', 'expert')), may hold values from 0.5 to 2
- out_grad: bfloat16 [16384, 2048], P(('dp', 'expert'), 'tensor'), may hold values from -1.5 to 1.5
- expert_ids: int32 [16384, 8], P(('dp', 'expert')), may hold values from 0 to 127, all different within a row; in each aligned block of 128 rows (0 to 127, 128 to 255, ...) at most 8 rows name the same one
- gates: float32 [16384, 8], P(('dp', 'expert')), may hold values from 0.05 to 1
- w_gate: bfloat16 [128, 768, 2048], P(('dp', 'expert'), 'tensor'), may hold values from -0.125 to 0.125
- w_up: bfloat16 [128, 768, 2048], P(('dp', 'expert'), 'tensor'), may hold values from -0.125 to 0.125
- w_down: bfloat16 [128, 768, 2048], P(('dp', 'expert'), 'tensor'), may hold values from -0.21875 to 0.21875
Outputs:
- grad_input: bfloat16 [16384, 2048], P(('dp', 'expert'), 'tensor')
- grad_gates: float32 [16384, 8], P(('dp', 'expert'))
Inputs may be any that keep to these rules, and one draw needn't show every extreme that they name: `expert_ids`: each row names 8 different experts. Among the 128 rows of one device (aligned blocks of rows), no expert is named more than 8 times, a bound that some block reaches.
All inputs are finite; a program needn't handle non-finite values.
Results may differ from a plain program's by a relative error of at most 0.012.
Values may be sent and summed in bfloat16 or wider, within the bound.
A program may use at most 64 MiB of HBM per device.

v0:
```python
import jax
import jax.numpy as jnp
from jax import lax
from jax.sharding import PartitionSpec as P


def body(checkpoint, scales, out_grad, expert_ids, gates, w_gate, w_up, w_down):
    f32, bf16 = (jnp.float32, jnp.bfloat16)
    planes = lax.axis_size("tensor")
    experts = lax.axis_size("dp") * lax.axis_size("expert")
    rank = lax.axis_index("tensor")
    tokens, part = checkpoint.shape
    picks = expert_ids.shape[1]
    cap = tokens * picks // experts
    own = cap // planes
    width = part * planes
    wg = lax.all_gather(w_gate[0], "tensor", axis=0, tiled=True)
    wu = lax.all_gather(w_up[0], "tensor", axis=0, tiled=True)
    wd = lax.all_gather(w_down[0], "tensor", axis=0, tiled=True)
    dequant = (checkpoint.astype(f32) * scales[:, None]).astype(bf16)
    both = lax.all_gather(jnp.stack([dequant, out_grad]), "tensor", axis=2, tiled=True)
    named = expert_ids[:, :, None] == jnp.arange(experts, dtype=jnp.int32)[None, None, :]
    member = jnp.any(named, axis=1)
    weight = jnp.sum(jnp.where(named, gates[:, :, None], 0.0), axis=1)
    lower = (jnp.arange(tokens)[:, None] > jnp.arange(tokens)[None, :]).astype(bf16)
    place = jnp.dot(lower, member.astype(bf16), preferred_element_type=f32).astype(jnp.int32)
    slots = rank * own + jnp.arange(own, dtype=jnp.int32)
    pick = member.T[:, None, :] & (place.T[:, None, :] == slots[None, :, None])
    pick_rows = pick.reshape(experts * own, tokens)
    one = pick_rows.astype(bf16)
    send_x = jnp.dot(one, both[0], preferred_element_type=f32).astype(bf16)
    send_g = jnp.dot(one, both[1], preferred_element_type=f32).astype(bf16)
    names = ("dp", "expert")
    rows = lax.all_to_all(send_x.reshape(experts, own, width), names, 0, 0, tiled=True)
    grads = lax.all_to_all(send_g.reshape(experts, own, width), names, 0, 0, tiled=True)
    rows = rows.reshape(experts * own, width)
    grads = grads.reshape(experts * own, width)
    contract = (((1,), (1,)), ((), ()))
    gate_pre = lax.dot_general(rows, wg, contract, preferred_element_type=f32)
    up_pre = lax.dot_general(rows, wu, contract, preferred_element_type=f32)
    back = lax.dot_general(grads, wd, contract, preferred_element_type=f32)
    sigma = jax.nn.sigmoid(gate_pre)
    swish = gate_pre * sigma
    hidden = (swish * up_pre).astype(bf16)
    gate_term = jnp.sum(hidden.astype(f32) * back, axis=1)
    d_gate = (back * up_pre * sigma * (1.0 + gate_pre * (1.0 - sigma))).astype(bf16)
    d_up = (back * swish).astype(bf16)
    result = jnp.dot(d_gate, wg, preferred_element_type=f32)
    result = result + jnp.dot(d_up, wu, preferred_element_type=f32)
    tail = jnp.broadcast_to(gate_term[:, None], (experts * own, 128))
    packed = jnp.concatenate([result.astype(bf16), tail.astype(bf16)], axis=1)
    came = lax.all_to_all(packed.reshape(experts, own, width + 128), names, 0, 0, tiled=True)
    came = came.reshape(experts * own, width + 128)
    combine = jnp.where(pick, weight.T[:, None, :], 0.0).reshape(experts * own, tokens)
    high = combine.astype(bf16)
    low = (combine - high.astype(f32)).astype(bf16)
    flip = (((0,), (0,)), ((), ()))
    mixed = lax.dot_general(high, came[:, :width], flip, preferred_element_type=f32)
    mixed = mixed + lax.dot_general(low, came[:, :width], flip, preferred_element_type=f32)
    term = jnp.sum(
        jnp.where(pick, came[:, width].astype(f32).reshape(experts, own)[:, :, None], 0.0), axis=1
    )
    terms = jnp.sum(jnp.where(named, term.T[:, None, :], 0.0), axis=2)
    terms = jnp.pad(terms, ((0, 0), (0, 128 - picks))).astype(bf16)
    joined = jnp.concatenate(
        [
            mixed.astype(bf16).reshape(tokens, planes, part),
            jnp.broadcast_to(terms[:, None], (tokens, planes, 128)),
        ],
        axis=2,
    ).transpose(1, 0, 2)
    summed = lax.psum_scatter(joined, "tensor", scatter_dimension=0, tiled=True)[0]
    return (summed[:, :part], summed[:, part : part + picks].astype(f32))


def solution(mesh):
    return jax.shard_map(
        body,
        mesh=mesh,
        in_specs=(
            P(("dp", "expert"), "tensor"),
            P(("dp", "expert")),
            P(("dp", "expert"), "tensor"),
            P(("dp", "expert"), None),
            P(("dp", "expert"), None),
            P(("dp", "expert"), "tensor", None),
            P(("dp", "expert"), "tensor", None),
            P(("dp", "expert"), "tensor", None),
        ),
        out_specs=(P(("dp", "expert"), "tensor"), P(("dp", "expert"), None)),
        check_vma=False,
    )
```

profile of v0, /device:TPU:8, one launch (start us, length us, event | category | flops | bytes accessed | tf_op | source)
XLA Modules:
  0.0 274.9 jit_solution(13853421694187391772)
XLA Ops:
  7.2 1.0 fusion.24
  8.2 1.6 pad_maximum_fusion.1
  9.9 0.7 all-gather.14.cloned.1.call-update
  10.7 0.7 all-gather.12.cloned.1.call-update
  12.3 31.8 %all-gather.8.cloned.1.call-done = bf16[2,128,2048]{2,1,0:T(8,128)(2,1)} async-done(((bf16[2,128,512]{2,1,0:T(8,128)(2,1)}), bf16[2,128,2048]{2,1,0:T(8,128)(2,1)}) %all-gather.8.cloned.1.call-update) | async-done | bytes 1048592 | tf_op jit(solution)/shard_map/all_gather | solution.py:21
  44.1 1.5 convolution_convert_fusion
  45.6 1.5 reshape.113
  47.1 14.2 %all-to-all-start.1 = ((bf16[128,2,2048]{2,1,0:T(2,128)(2,1)}), bf16[128,2,2048]{2,1,0:T(2,128)(2,1)S(1)}, u32[]{:S(2)}, u32[]{:S(2)}) async-start(bf16[128,2,2048]{2,1,0:T(2,128)(2,1)} %reshape.113), calls=%async_computation.1 | async-start | bytes 2097152 | tf_op jit(solution)/shard_map/all_to_all | solution.py:34
  61.3 0.5 all-gather.10.cloned.1.call-update
  62.3 1.5 reshape.111
  63.8 28.5 %all-to-all-done.1 = bf16[128,2,2048]{2,1,0:T(2,128)(2,1)S(1)} async-done(((bf16[128,2,2048]{2,1,0:T(2,128)(2,1)}), bf16[128,2,2048]{2,1,0:T(2,128)(2,1)S(1)}, u32[]{:S(2)}, u32[]{:S(2)}) %all-to-all-start.1) | async-done | bytes 1048608 | tf_op jit(solution)/shard_map/all_to_all | solution.py:34
  92.2 7.5 %all-to-all-start = ((bf16[128,2,2048]{2,1,0:T(2,128)(2,1)}), bf16[128,2,2048]{2,1,0:T(2,128)(2,1)S(1)}, u32[]{:S(2)}, u32[]{:S(2)}) async-start(bf16[128,2,2048]{2,1,0:T(2,128)(2,1)} %reshape.111), calls=%async_computation | async-start | bytes 2097152 | tf_op jit(solution)/shard_map/all_to_all | solution.py:35
  99.7 0.4 reshape.114
  100.2 30.6 %all-to-all-done = bf16[128,2,2048]{2,1,0:T(2,128)(2,1)S(1)} async-done(((bf16[128,2,2048]{2,1,0:T(2,128)(2,1)}), bf16[128,2,2048]{2,1,0:T(2,128)(2,1)S(1)}, u32[]{:S(2)}, u32[]{:S(2)}) %all-to-all-start) | async-done | bytes 1048608 | tf_op jit(solution)/shard_map/all_to_all | solution.py:35
  131.2 3.0 %fusion.2 = f32[256,768]{1,0:T(8,128)S(1)} fusion(bf16[256,2048]{1,0:T(8,128)(2,1)S(1)} %reshape.114, bf16[1,768,2048]{2,1,0:T(8,128)(2,1)} %all-gather.14.cloned.1.call-done), kind=kOutput, calls=%fused_computation.2 | convolution fusion | flops 805306368 | bytes 4980736 | tf_op jit(solution)/shard_map/dot_general | solution.py:39
  134.3 4.4 %all-gather.12.cloned.1.call-done = bf16[1,768,2048]{2,1,0:T(8,128)(2,1)} async-done(((bf16[1,192,2048]{2,1,0:T(8,128)(2,1)}), bf16[1,768,2048]{2,1,0:T(8,128)(2,1)}) %all-gather.12.cloned.1.call-update) | async-done | bytes 3145744 | tf_op jit(solution)/shard_map/all_gather | solution.py:18
  138.6 3.9 %fusion.6 = f32[256,768]{1,0:T(8,128)} fusion(bf16[256,2048]{1,0:T(8,128)(2,1)S(1)} %reshape.114, bf16[1,768,2048]{2,1,0:T(8,128)(2,1)} %all-gather.12.cloned.1.call-done), kind=kOutput, calls=%fused_computation.6 | convolution fusion | flops 805306368 | bytes 4980736 | tf_op jit(solution)/shard_map/dot_general | solution.py:40
  142.5 43.1 %all-gather.10.cloned.1.call-done = bf16[1,768,2048]{2,1,0:T(8,128)(2,1)} async-done(((bf16[1,192,2048]{2,1,0:T(8,128)(2,1)}), bf16[1,768,2048]{2,1,0:T(8,128)(2,1)}) %all-gather.10.cloned.1.call-update) | async-done | bytes 3145744 | tf_op jit(solution)/shard_map/all_gather | solution.py:19
  185.7 3.4 %multiply_reduce_fusion = (bf16[256]{0:T(256)(128)(2,1)S(1)}, f32[256,768]{1,0:T(8,128)S(1)}) fusion(f32[256,768]{1,0:T(8,128)} %fusion.6, f32[256,768]{1,0:T(8,128)S(1)} %fusion.2, bf16[256,2048]{1,0:T(8,128)(2,1)S(1)} %reshape.112, bf16[1,768,2048]{2,1,0:T(8,128)(2,1)} %all-gather.10.cloned.1.call-done), kind=kOutput, calls=%fused_computation.21 | convolution fusion | flops 807075584 | bytes 6554112 | tf_op jit(solution)/shard_map/dot_general | solution.py:41
  189.1 1.2 fusion
  190.3 0.7 copy-done.4
  191.0 1.1 fusion.13
  192.3 1.3 reshape.115
  193.5 14.3 %all-to-all-start.2 = ((bf16[128,2,2176]{2,1,0:T(2,128)(2,1)}), bf16[128,2,2176]{2,1,0:T(2,128)(2,1)S(1)}, u32[]{:S(2)}, u32[]{:S(2)}) async-start(bf16[128,2,2176]{2,1,0:T(2,128)(2,1)} %reshape.115), calls=%async_computation.2 | async-start | bytes 2228224 | tf_op jit(solution)/shard_map/all_to_all | solution.py:52
  208.4 32.1 %all-to-all-done.2 = bf16[128,2,2176]{2,1,0:T(2,128)(2,1)S(1)} async-done(((bf16[128,2,2176]{2,1,0:T(2,128)(2,1)}), bf16[128,2,2176]{2,1,0:T(2,128)(2,1)S(1)}, u32[]{:S(2)}, u32[]{:S(2)}) %all-to-all-start.2) | async-done | bytes 1114144 | tf_op jit(solution)/shard_map/all_to_all | solution.py:52
  240.4 0.4 reshape.116
  241.6 0.5 select_reduce_fusion.1
  243.6 0.9 maximum_bitcast_fusion
  244.5 21.0 %reduce-scatter.2.cloned.1.call-done = bf16[1,128,640]{1,2,0:T(8,128)(2,1)} async-done(((bf16[4,128,640]{1,2,0:T(8,128)(2,1)}), bf16[1,128,640]{1,2,0:T(8,128)(2,1)}) %reduce-scatter.2.cloned.1.call-update) | async-done | bytes 163856 | tf_op jit(solution)/shard_map/reduce_scatter | solution.py:72
  265.5 0.9 slice.29
  266.4 1.3 slice_convert_fusion
  267.6 0.8 copy.36
  (48 shorter events, 4.7 us)
Async XLA Ops:
  7.2 4.2 %copy-start.1 = (s32[128,8]{0,1:T(8,128)S(1)}, s32[128,8]{0,1:T(8,128)}, u32[]{:S(2)}) copy-start(s32[128,8]{0,1:T(8,128)} %param.11) | copy-start | bytes 12292
  7.2 36.9 %all-gather.8.cloned.1.call-start = ((), (), s32[]{:S(2)}) async-start(), calls=%async_computation.4 | async-start | bytes 1310720 | tf_op jit(solution)/shard_map/all_gather | solution.py:21
  9.9 121.3 %all-gather.14.cloned.1.call-start = ((), (), s32[]{:S(2)}) async-start(), calls=%async_computation.8 | async-start | bytes 3932160 | tf_op jit(solution)/shard_map/all_gather | solution.py:17
  10.6 128.0 %all-gather.12.cloned.1.call-start = ((), (), s32[]{:S(2)}) async-start(), calls=%async_computation.7 | async-start | bytes 3932160 | tf_op jit(solution)/shard_map/all_gather | solution.py:18
  45.6 16.2 %copy-start = (bf16[2,128,2048]{2,1,0:T(8,128)(2,1)S(1)}, bf16[2,128,2048]{2,1,0:T(8,128)(2,1)}, u32[]{:S(2)}) copy-start(bf16[2,128,2048]{2,1,0:T(8,128)(2,1)} %all-gather.8.cloned.1.call-done) | copy-start | bytes 3145732
  47.1 45.2 %all-to-all-start.1 = ((bf16[128,2,2048]{2,1,0:T(2,128)(2,1)}), bf16[128,2,2048]{2,1,0:T(2,128)(2,1)S(1)}, u32[]{:S(2)}, u32[]{:S(2)}) async-start(bf16[128,2,2048]{2,1,0:T(2,128)(2,1)} %reshape.113), calls=%async_computation.1 | async-start | bytes 2097152 | tf_op jit(solution)/shard_map/all_to_all | solution.py:34
  61.2 124.4 %all-gather.10.cloned.1.call-start = ((), (), s32[]{:S(2)}) async-start(), calls=%async_computation.6 | async-start | bytes 3932160 | tf_op jit(solution)/shard_map/all_gather | solution.py:19
  92.2 38.5 %all-to-all-start = ((bf16[128,2,2048]{2,1,0:T(2,128)(2,1)}), bf16[128,2,2048]{2,1,0:T(2,128)(2,1)S(1)}, u32[]{:S(2)}, u32[]{:S(2)}) async-start(bf16[128,2,2048]{2,1,0:T(2,128)(2,1)} %reshape.111), calls=%async_computation | async-start | bytes 2097152 | tf_op jit(solution)/shard_map/all_to_all | solution.py:35
  185.7 3.4 %copy-start.3 = (bf16[1,768,2048]{2,1,0:T(8,128)(2,1)S(1)}, bf16[1,768,2048]{2,1,0:T(8,128)(2,1)}, u32[]{:S(2)}) copy-start(bf16[1,768,2048]{2,1,0:T(8,128)(2,1)} %all-gather.14.cloned.1.call-done) | copy-start | bytes 9437188
  185.7 3.4 %copy-start.5 = (f32[256,768]{1,0:T(8,128)S(1)}, f32[256,768]{1,0:T(8,128)}, u32[]{:S(2)}) copy-start(f32[256,768]{1,0:T(8,128)} %fusion.6) | copy-start | bytes 2359300
  189.1 1.9 copy-start.4
  192.3 15.7 %copy-start.2 = (f32[128,8]{0,1:T(8,128)S(1)}, f32[128,8]{0,1:T(8,128)}, u32[]{:S(2)}) copy-start(f32[128,8]{0,1:T(8,128)} %param.12) | copy-start | bytes 12292
  193.5 46.9 %all-to-all-start.2 = ((bf16[128,2,2176]{2,1,0:T(2,128)(2,1)}), bf16[128,2,2176]{2,1,0:T(2,128)(2,1)S(1)}, u32[]{:S(2)}, u32[]{:S(2)}) async-start(bf16[128,2,2176]{2,1,0:T(2,128)(2,1)} %reshape.115), calls=%async_computation.2 | async-start | bytes 2228224 | tf_op jit(solution)/shard_map/all_to_all | solution.py:52
  207.9 57.6 %reduce-scatter.2.cloned.1.call-start = ((), (), s32[]{:S(2)}) async-start(), calls=%async_computation.5 | async-start | bytes 819200 | tf_op jit(solution)/shard_map/reduce_scatter | solution.py:72
Sparse Core Ops, SparseCore 0:
  10.1 33.9 all-gather.7
  46.2 45.2 all-gather.13
  93.6 45.0 all-gather.11
  140.6 45.0 all-gather.9
  244.6 20.8 reduce-scatter.1
where the time goes:
time: 276 us; the launch traced here: 275 us
  waiting for transfers between devices  193 us (70%)
  starting transfers between devices  36.2 us (13%)
  matrix products  15.5 us (6%)
  between operations  14.1 us (5%)
  local copies, waits for them, and re-layouts  9.56 us (3%)
  other arithmetic  6.24 us (2%)
    all_gather x1, waiting for transfers between devices, body(): wd = lax.all_gather(w_down[0], 'tensor', axis=0, tiled=True)  43.1 us
    all_to_all x1, waiting for transfers between devices, body(): lax.all_to_all(packed.reshape(experts, own, width + 128), names, 0, 0, ti...  32.1 us
    all_gather x1, waiting for transfers between devices, body(): lax.all_gather(jnp.stack([dequant, out_grad]), 'tensor', axis=2, tiled=True)  31.8 us
    all_to_all x1, waiting for transfers between devices, body(): lax.all_to_all(send_g.reshape(experts, own, width), names, 0, 0, tiled=True)  30.6 us
    all_to_all x1, waiting for transfers between devices, body(): lax.all_to_all(send_x.reshape(experts, own, width), names, 0, 0, tiled=True)  28.5 us
    reduce_scatter x1, waiting for transfers between devices, body(): lax.psum_scatter(joined, 'tensor', scatter_dimension=0, tiled=True)[0]  21 us
    all_to_all x1, starting transfers between devices, body(): lax.all_to_all(packed.reshape(experts, own, width + 128), names, 0, 0, ti...  14.3 us
    all_to_all x1, starting transfers between devices, body(): lax.all_to_all(send_x.reshape(experts, own, width), names, 0, 0, tiled=True)  14.2 us
  transfers between devices with their start and end apart: 8, of which 7 were waited for; matrix products, arithmetic and copies ran while one was open for 5% of the time, Pallas kernels for 0%

commit v1 on v0

--- a/solution.py
+++ b/solution.py
@@ -18,7 +18,9 @@
     wu = lax.all_gather(w_up[0], "tensor", axis=0, tiled=True)
     wd = lax.all_gather(w_down[0], "tensor", axis=0, tiled=True)
     dequant = (checkpoint.astype(f32) * scales[:, None]).astype(bf16)
-    both = lax.all_gather(jnp.stack([dequant, out_grad]), "tensor", axis=2, tiled=True)
+    shard = jnp.stack([dequant, out_grad])
+    copies = jnp.concatenate([shard] * lax.axis_size("tensor"), axis=2)
+    both = lax.all_to_all(copies, "tensor", 2, 2, tiled=True)
     named = expert_ids[:, :, None] == jnp.arange(experts, dtype=jnp.int32)[None, None, :]
     member = jnp.any(named, axis=1)
     weight = jnp.sum(jnp.where(named, gates[:, :, None], 0.0), axis=1)

time: 276 us -> 244 us (0.88)
  waiting for transfers between devices: 193 us -> 145 us
  starting transfers between devices: 36.2 us -> 48.4 us
  local copies, waits for them, and re-layouts: 9.56 us -> 15.5 us
    all_gather x1 -> x0, waiting for transfers between devices: 31.8 us -> none  [body(): lax.all_gather(jnp.stack([dequant, out_grad]), 'tensor', axis=2, tiled=True)]
    all_gather x1, waiting for transfers between devices: 43.1 us -> 17.1 us  [body(): wd = lax.all_gather(w_down[0], 'tensor', axis=0, tiled=True)]
    all_to_all x0 -> x1, waiting for transfers between devices: none -> 14.1 us  [body(): both = lax.all_to_all(copies, 'tensor', 2, 2, tiled=True)]
    all_to_all x1, starting transfers between devices: 14.2 us -> 22.3 us  [body(): lax.all_to_all(send_x.reshape(experts, own, width), names, 0, 0, tiled=True)]
    all_gather x1, waiting for transfers between devices: 4.39 us -> 0.02 us  [body(): wu = lax.all_gather(w_up[0], 'tensor', axis=0, tiled=True)]
    all_to_all x0 -> x1, starting transfers between devices: none -> 4.29 us  [body(): both = lax.all_to_all(copies, 'tensor', 2, 2, tiled=True)]
  transfers between devices with their start and end apart: 8 -> 8, of which waited for: 7 -> 6; matrix products, arithmetic and copies ran while one was open for 5% -> 9% of each run, Pallas kernels for 0% -> 0%
where the time goes in v1:
time: 244 us
  waiting for transfers between devices  145 us (59%)
  starting transfers between devices  48.4 us (20%)
  local copies, waits for them, and re-layouts  15.5 us (6%)
  matrix products  15.3 us (6%)
  between operations  14.1 us (6%)
  other arithmetic  5.86 us (2%)
    all_to_all x1, waiting for transfers between devices, body(): lax.all_to_all(packed.reshape(experts, own, width + 128), names, 0, 0, ti...  32.1 us
    all_to_all x1, waiting for transfers between devices, body(): lax.all_to_all(send_g.reshape(experts, own, width), names, 0, 0, tiled=True)  30.5 us
    all_to_all x1, waiting for transfers between devices, body(): lax.all_to_all(send_x.reshape(experts, own, width), names, 0, 0, tiled=True)  27.6 us
    all_to_all x1, starting transfers between devices, body(): lax.all_to_all(send_x.reshape(experts, own, width), names, 0, 0, tiled=True)  22.3 us
    reduce_scatter x1, waiting for transfers between devices, body(): lax.psum_scatter(joined, 'tensor', scatter_dimension=0, tiled=True)[0]  21 us
    all_gather x1, waiting for transfers between devices, body(): wd = lax.all_gather(w_down[0], 'tensor', axis=0, tiled=True)  17.1 us
    all_to_all x1, starting transfers between devices, body(): lax.all_to_all(packed.reshape(experts, own, width + 128), names, 0, 0, ti...  14.2 us
    all_to_all x1, waiting for transfers between devices, body(): both = lax.all_to_all(copies, 'tensor', 2, 2, tiled=True)  14.1 us
  transfers between devices with their start and end apart: 8, of which 6 were waited for; matrix products, arithmetic and copies ran while one was open for 9% of the time, Pallas kernels for 0%

profile of v1, /device:TPU:8, one launch (start us, length us, event | category | flops | bytes accessed | tf_op | source)
XLA Modules:
  0.0 243.8 jit_solution(4451182383812357290)
XLA Ops:
  7.2 0.7 all-gather.11.cloned.1.call-update
  7.9 0.7 all-gather.9.cloned.1.call-update
  8.6 1.0 fusion.26
  9.6 1.3 maximum_maximum_fusion
  10.9 2.0 copy.43
  12.9 4.3 %all-to-all-start = ((bf16[2,128,2048]{1,0,2:T(2,128)(2,1)}), bf16[2,128,2048]{1,0,2:T(2,128)(2,1)S(1)}, u32[]{:S(2)}, u32[]{:S(2)}) async-start(bf16[2,128,2048]{1,0,2:T(2,128)(2,1)} %copy.43), calls=%async_computation | async-start | bytes 2097152 | tf_op jit(solution)/shard_map/all_to_all | solution.py:23
  18.2 14.1 %all-to-all-done = bf16[2,128,2048]{1,0,2:T(2,128)(2,1)S(1)} async-done(((bf16[2,128,2048]{1,0,2:T(2,128)(2,1)}), bf16[2,128,2048]{1,0,2:T(2,128)(2,1)S(1)}, u32[]{:S(2)}, u32[]{:S(2)}) %all-to-all-start) | async-done | bytes 1048608 | tf_op jit(solution)/shard_map/all_to_all | solution.py:23
  32.3 1.5 fusion.32
  33.8 1.8 copy.52
  35.6 1.5 convolution_convert_fusion
  37.1 1.5 reshape.113
  38.6 22.3 %all-to-all-start.2 = ((bf16[128,2,2048]{2,1,0:T(2,128)(2,1)}), bf16[128,2,2048]{2,1,0:T(2,128)(2,1)S(1)}, u32[]{:S(2)}, u32[]{:S(2)}) async-start(bf16[128,2,2048]{2,1,0:T(2,128)(2,1)} %reshape.113), calls=%async_computation.2 | async-start | bytes 2097152 | tf_op jit(solution)/shard_map/all_to_all | solution.py:36
  60.9 0.7 all-gather.7.cloned.1.call-update
  62.7 1.5 reshape.111
  64.2 27.6 %all-to-all-done.2 = bf16[128,2,2048]{2,1,0:T(2,128)(2,1)S(1)} async-done(((bf16[128,2,2048]{2,1,0:T(2,128)(2,1)}), bf16[128,2,2048]{2,1,0:T(2,128)(2,1)S(1)}, u32[]{:S(2)}, u32[]{:S(2)}) %all-to-all-start.2) | async-done | bytes 1048608 | tf_op jit(solution)/shard_map/all_to_all | solution.py:36
  91.9 7.5 %all-to-all-start.1 = ((bf16[128,2,2048]{2,1,0:T(2,128)(2,1)}), bf16[128,2,2048]{2,1,0:T(2,128)(2,1)S(1)}, u32[]{:S(2)}, u32[]{:S(2)}) async-start(bf16[128,2,2048]{2,1,0:T(2,128)(2,1)} %reshape.111), calls=%async_computation.1 | async-start | bytes 2097152 | tf_op jit(solution)/shard_map/all_to_all | solution.py:37
  99.8 30.5 %all-to-all-done.1 = bf16[128,2,2048]{2,1,0:T(2,128)(2,1)S(1)} async-done(((bf16[128,2,2048]{2,1,0:T(2,128)(2,1)}), bf16[128,2,2048]{2,1,0:T(2,128)(2,1)S(1)}, u32[]{:S(2)}, u32[]{:S(2)}) %all-to-all-start.1) | async-done | bytes 1048608 | tf_op jit(solution)/shard_map/all_to_all | solution.py:37
  130.8 2.9 %fusion.2 = f32[256,768]{1,0:T(8,128)S(1)} fusion(bf16[256,2048]{1,0:T(8,128)(2,1)S(1)} %reshape.114, bf16[1,768,2048]{2,1,0:T(8,128)(2,1)} %all-gather.11.cloned.1.call-done), kind=kOutput, calls=%fused_computation.2 | convolution fusion | flops 805306368 | bytes 4980736 | tf_op jit(solution)/shard_map/dot_general | solution.py:41
  133.8 3.8 %fusion.6 = f32[256,768]{1,0:T(8,128)} fusion(bf16[256,2048]{1,0:T(8,128)(2,1)S(1)} %reshape.114, bf16[1,768,2048]{2,1,0:T(8,128)(2,1)} %all-gather.9.cloned.1.call-done), kind=kOutput, calls=%fused_computation.6 | convolution fusion | flops 805306368 | bytes 4980736 | tf_op jit(solution)/shard_map/dot_general | solution.py:42
  137.6 17.1 %all-gather.7.cloned.1.call-done = bf16[1,768,2048]{2,1,0:T(8,128)(2,1)} async-done(((bf16[1,192,2048]{2,1,0:T(8,128)(2,1)}), bf16[1,768,2048]{2,1,0:T(8,128)(2,1)}) %all-gather.7.cloned.1.call-update) | async-done | bytes 3145744 | tf_op jit(solution)/shard_map/all_gather | solution.py:19
  154.8 3.4 %multiply_reduce_fusion = (bf16[256]{0:T(256)(128)(2,1)S(1)}, f32[256,768]{1,0:T(8,128)S(1)}) fusion(f32[256,768]{1,0:T(8,128)} %fusion.6, f32[256,768]{1,0:T(8,128)S(1)} %fusion.2, bf16[256,2048]{1,0:T(8,128)(2,1)S(1)} %reshape.112, bf16[1,768,2048]{2,1,0:T(8,128)(2,1)} %all-gather.7.cloned.1.call-done), kind=kOutput, calls=%fused_computation.22 | convolution fusion | flops 807075584 | bytes 6554112 | tf_op jit(solution)/shard_map/dot_general | solution.py:43
  158.2 1.2 fusion
  159.4 0.7 copy-done.3
  160.1 1.1 fusion.13
  161.4 1.2 reshape.115
  162.6 14.2 %all-to-all-start.3 = ((bf16[128,2,2176]{2,1,0:T(2,128)(2,1)}), bf16[128,2,2176]{2,1,0:T(2,128)(2,1)S(1)}, u32[]{:S(2)}, u32[]{:S(2)}) async-start(bf16[128,2,2176]{2,1,0:T(2,128)(2,1)} %reshape.115), calls=%async_computation.3 | async-start | bytes 2228224 | tf_op jit(solution)/shard_map/all_to_all | solution.py:54
  177.3 32.1 %all-to-all-done.3 = bf16[128,2,2176]{2,1,0:T(2,128)(2,1)S(1)} async-done(((bf16[128,2,2176]{2,1,0:T(2,128)(2,1)}), bf16[128,2,2176]{2,1,0:T(2,128)(2,1)S(1)}, u32[]{:S(2)}, u32[]{:S(2)}) %all-to-all-start.3) | async-done | bytes 1114144 | tf_op jit(solution)/shard_map/all_to_all | solution.py:54
  212.5 0.9 maximum_bitcast_fusion
  213.4 21.0 %reduce-scatter.2.cloned.1.call-done = bf16[1,128,640]{1,2,0:T(8,128)(2,1)} async-done(((bf16[4,128,640]{1,2,0:T(8,128)(2,1)}), bf16[1,128,640]{1,2,0:T(8,128)(2,1)}) %reduce-scatter.2.cloned.1.call-update) | async-done | bytes 163856 | tf_op jit(solution)/shard_map/reduce_scatter | solution.py:74
  234.4 0.9 slice.29
  235.3 1.3 slice_convert_fusion
  236.5 0.8 copy.49
  (49 shorter events, 6.7 us)
Async XLA Ops:
  7.2 123.7 %all-gather.11.cloned.1.call-start = ((), (), s32[]{:S(2)}) async-start(), calls=%async_computation.8 | async-start | bytes 3932160 | tf_op jit(solution)/shard_map/all_gather | solution.py:17
  7.9 125.9 %all-gather.9.cloned.1.call-start = ((), (), s32[]{:S(2)}) async-start(), calls=%async_computation.7 | async-start | bytes 3932160 | tf_op jit(solution)/shard_map/all_gather | solution.py:18
  10.9 6.3 %copy-start = (s32[128,8]{0,1:T(8,128)S(1)}, s32[128,8]{0,1:T(8,128)}, u32[]{:S(2)}) copy-start(s32[128,8]{0,1:T(8,128)} %param.11) | copy-start | bytes 12292
  12.9 19.4 %all-to-all-start = ((bf16[2,128,2048]{1,0,2:T(2,128)(2,1)}), bf16[2,128,2048]{1,0,2:T(2,128)(2,1)S(1)}, u32[]{:S(2)}, u32[]{:S(2)}) async-start(bf16[2,128,2048]{1,0,2:T(2,128)(2,1)} %copy.43), calls=%async_computation | async-start | bytes 2097152 | tf_op jit(solution)/shard_map/all_to_all | solution.py:23
  38.6 53.3 %all-to-all-start.2 = ((bf16[128,2,2048]{2,1,0:T(2,128)(2,1)}), bf16[128,2,2048]{2,1,0:T(2,128)(2,1)S(1)}, u32[]{:S(2)}, u32[]{:S(2)}) async-start(bf16[128,2,2048]{2,1,0:T(2,128)(2,1)} %reshape.113), calls=%async_computation.2 | async-start | bytes 2097152 | tf_op jit(solution)/shard_map/all_to_all | solution.py:36
  60.9 93.9 %all-gather.7.cloned.1.call-start = ((), (), s32[]{:S(2)}) async-start(), calls=%async_computation.6 | async-start | bytes 3932160 | tf_op jit(solution)/shard_map/all_gather | solution.py:19
  91.9 38.5 %all-to-all-start.1 = ((bf16[128,2,2048]{2,1,0:T(2,128)(2,1)}), bf16[128,2,2048]{2,1,0:T(2,128)(2,1)S(1)}, u32[]{:S(2)}, u32[]{:S(2)}) async-start(bf16[128,2,2048]{2,1,0:T(2,128)(2,1)} %reshape.111), calls=%async_computation.1 | async-start | bytes 2097152 | tf_op jit(solution)/shard_map/all_to_all | solution.py:37
  154.8 3.4 %copy-start.2 = (bf16[1,768,2048]{2,1,0:T(8,128)(2,1)S(1)}, bf16[1,768,2048]{2,1,0:T(8,128)(2,1)}, u32[]{:S(2)}) copy-start(bf16[1,768,2048]{2,1,0:T(8,128)(2,1)} %all-gather.11.cloned.1.call-done) | copy-start | bytes 9437188
  154.8 3.4 %copy-start.4 = (f32[256,768]{1,0:T(8,128)S(1)}, f32[256,768]{1,0:T(8,128)}, u32[]{:S(2)}) copy-start(f32[256,768]{1,0:T(8,128)} %fusion.6) | copy-start | bytes 2359300
  158.2 1.9 copy-start.3
  161.4 15.5 %copy-start.1 = (f32[128,8]{0,1:T(8,128)S(1)}, f32[128,8]{0,1:T(8,128)}, u32[]{:S(2)}) copy-start(f32[128,8]{0,1:T(8,128)} %param.12) | copy-start | bytes 12292
  162.6 46.7 %all-to-all-start.3 = ((bf16[128,2,2176]{2,1,0:T(2,128)(2,1)}), bf16[128,2,2176]{2,1,0:T(2,128)(2,1)S(1)}, u32[]{:S(2)}, u32[]{:S(2)}) async-start(bf16[128,2,2176]{2,1,0:T(2,128)(2,1)} %reshape.115), calls=%async_computation.3 | async-start | bytes 2228224 | tf_op jit(solution)/shard_map/all_to_all | solution.py:54
  176.8 57.6 %reduce-scatter.2.cloned.1.call-start = ((), (), s32[]{:S(2)}) async-start(), calls=%async_computation.5 | async-start | bytes 819200 | tf_op jit(solution)/shard_map/reduce_scatter | solution.py:74
Sparse Core Ops, SparseCore 0:
  10.1 49.3 all-gather.10
  61.6 45.9 all-gather.8
  109.7 45.0 all-gather.6
  213.5 20.8 reduce-scatter.1
